TPU v7x, 32 devices: a whole 2x2x4 slice. The times are simulated.
32 devices in a mesh: dp: 8 (over z, x), tensor: 4 (over y, core).
Axes of the slice: x: 2, y: 2, z: 4, core: 2. Of those that a mesh axis runs over, the one named last changes fastest.
Arguments:
- tokens: bfloat16 [8192, 1024], P('dp')
- segments: int32 [8, 1024], P('dp'), may hold values from -1 to 16, as said below
- w_query: bfloat16 [1024, 1024], P(None, 'tensor'), may hold values from -0.1875 to 0.1875
- w_key: bfloat16 [1024, 1024], P(None, 'tensor'), may hold values from -0.1875 to 0.1875
- w_value: bfloat16 [1024, 1024], P(None, 'tensor'), may hold values from -0.1875 to 0.1875
- w_out: bfloat16 [1024, 1024], P(None, 'tensor'), may hold values from -0.1875 to 0.1875
- w_fc1: bfloat16 [1024, 4096], P(None, 'tensor'), may hold values from -0.1875 to 0.1875
- w_fc2: bfloat16 [1024, 4096], P(None, 'tensor'), may hold values from -0.09375 to 0.09375
- ln1_gain: float32 [1024], replicated, may hold values from 0.5 to 1.5
- ln1_bias: float32 [1024], replicated, may hold values from -1.2 to 1.2
- post_gain: float32 [1024], replicated, may hold values from 0.5 to 1.5
- post_bias: float32 [1024], replicated, may hold values from -1.2 to 1.2
- ln2_gain: float32 [1024], replicated, may hold values from 0.5 to 1.5
- ln2_bias: float32 [1024], replicated, may hold values from -1.2 to 1.2
- mid_gain: float32 [4096], P('tensor'), may hold values from 0.5 to 1.5
- mid_bias: float32 [4096], P('tensor'), may hold values from -1.2 to 1.2
- query_bias: float32 [1024], P('tensor'), may hold values from -1.2 to 1.2
- value_bias: float32 [1024], P('tensor'), may hold values from -1.2 to 1.2
- out_bias: float32 [1024], replicated, may hold values from -1.2 to 1.2
- fc1_bias: float32 [4096], P('tensor'), may hold values from -1.2 to 1.2
- fc2_bias: float32 [1024], replicated, may hold values from -1.2 to 1.2
- head_scale: float32 [16], P('tensor'), may hold values from 0.25 to 1.75
- cotangent: bfloat16 [8192, 1024], P('dp'), may hold values from -6 to 6
Outputs:
- output: bfloat16 [8192, 1024], P('dp')
- grad_tokens: float32 [8192, 1024], P('dp')
- grad_w_query: float32 [1024, 1024], P('dp', 'tensor')
- grad_w_key: float32 [1024, 1024], P('dp', 'tensor')
- grad_w_value: float32 [1024, 1024], P('dp', 'tensor')
- grad_w_out: float32 [1024, 1024], P('dp', 'tensor')
- grad_w_fc1: float32 [1024, 4096], P('dp', 'tensor')
- grad_w_fc2: float32 [1024, 4096], P('dp', 'tensor')
- grad_ln1_gain: float32 [1024], replicated
- grad_ln1_bias: float32 [1024], replicated
- grad_post_gain: float32 [1024], replicated
- grad_post_bias: float32 [1024], replicated
- grad_ln2_gain: float32 [1024], replicated
- grad_ln2_bias: float32 [1024], replicated
- grad_mid_gain: float32 [4096], P('tensor')
- grad_mid_bias: float32 [4096], P('tensor')
- grad_query_bias: float32 [1024], P('tensor')
- grad_value_bias: float32 [1024], P('tensor')
- grad_out_bias: float32 [1024], replicated
- grad_fc1_bias: float32 [4096], P('tensor')
- grad_fc2_bias: float32 [1024], replicated
- grad_head_scale: float32 [16], P('tensor')
- rms: float32 [3], replicated
Inputs may be any that keep to these rules, and one draw needn't show every extreme that they name: `segments`: each row of 1024 tokens holds whole documents of 60 to 800 tokens, numbered 0, 1, 2 and so on from the row's start, then padding marked -1 where the next document would not fit; the first document always fits. Some row holds only documents of 60 tokens followed by padding.
All inputs are finite; a program needn't handle non-finite values.
Results may differ from a plain program's by a relative error of at most 0.014.
Values sent between devices are 32-bit elements; how exact they have to be, the bound alone decides.
No kernel may reach another device: no remote copies, remote signals or barrier semaphores. Data moves between devices by JAX's collectives and lax.ppermute only.
A program may use at most 128 MiB of HBM per device.

v0:
```python
import jax
import jax.numpy as jnp
from jax import lax
from jax.sharding import PartitionSpec as P

D = 1024
HEAD_DIM = 64
FF = 4096
epsilon = 1e-05


def normalize(v):
    mean = jnp.mean(v, axis=-1, keepdims=True)
    centred = v - mean
    factor = lax.rsqrt(jnp.mean(centred * centred, axis=-1, keepdims=True) + epsilon)
    return (centred * factor, factor)


def norm_back(scaled, normed, factor):
    return factor * (
        scaled
        - jnp.mean(scaled, axis=-1, keepdims=True)
        - normed * jnp.mean(scaled * normed, axis=-1, keepdims=True)
    )


def project(left, right):
    return jnp.dot(left, right, preferred_element_type=jnp.float32)


def project_t(left, right):
    return lax.dot_general(
        left, right, (((1,), (1,)), ((), ())), preferred_element_type=jnp.float32
    )


def outer_sum(left, right):
    return lax.dot_general(
        left, right, (((0,), (0,)), ((), ())), preferred_element_type=jnp.float32
    )


def gelu_tanh(v):
    return jax.nn.gelu(v, approximate=True)


def block_scores(query_rows, keys, seg_rows, seg_keys, first):
    scores = jnp.einsum(
        "qhd,khd->hqk", query_rows, keys, preferred_element_type=jnp.float32
    ) * HEAD_DIM ** (-0.5)
    places = first + jnp.arange(query_rows.shape[0])
    allowed = (seg_rows[:, None] == seg_keys[None, :]) & (
        jnp.arange(keys.shape[0])[None, :] <= places[:, None]
    )
    return jnp.where(allowed[None], scores, -1e30)


def attend(query4, key4, value4, segments, block):
    length = query4.shape[1]
    count = length // block

    def per_sequence(item):
        queries, keys, values, seg = item

        def per_block(index):
            first = index * block
            rows_q = lax.dynamic_slice_in_dim(queries, first, block, 0)
            rows_seg = lax.dynamic_slice_in_dim(seg, first, block, 0)
            scores = block_scores(rows_q, keys, rows_seg, seg, first)
            top = jnp.max(scores, axis=-1, keepdims=True)
            expo = jnp.exp(scores - top)
            total = jnp.sum(expo, axis=-1, keepdims=True)
            weights = (expo / total).astype(jnp.bfloat16)
            result = jnp.einsum("hqk,khd->qhd", weights, values, preferred_element_type=jnp.float32)
            return (result, (top + jnp.log(total))[..., 0])

        results, logsum = lax.map(per_block, jnp.arange(count))
        return (results.reshape(length, results.shape[2], results.shape[3]), logsum)

    return lax.map(per_sequence, (query4, key4, value4, segments))


def attend_back(query4, key4, value4, segments, logsum, grad4, block):
    length = query4.shape[1]
    count = length // block
    factor = HEAD_DIM ** (-0.5)

    def per_sequence(item):
        queries, keys, values, seg, seq_logsum, grads = item

        def per_block(carry, index):
            key_grad, value_grad = carry
            first = index * block
            rows_q = lax.dynamic_slice_in_dim(queries, first, block, 0)
            rows_seg = lax.dynamic_slice_in_dim(seg, first, block, 0)
            rows_grad = lax.dynamic_slice_in_dim(grads, first, block, 0)
            scores = block_scores(rows_q, keys, rows_seg, seg, first)
            probs = jnp.exp(scores - seq_logsum[index][..., None])
            weights = probs.astype(jnp.bfloat16)
            value_grad = value_grad + jnp.einsum(
                "hqk,qhd->khd", weights, rows_grad, preferred_element_type=jnp.float32
            )
            prob_grad = jnp.einsum(
                "qhd,khd->hqk", rows_grad, values, preferred_element_type=jnp.float32
            )
            along = jnp.sum(probs * prob_grad, axis=-1, keepdims=True)
            score_grad = (probs * (prob_grad - along)).astype(jnp.bfloat16)
            query_grad = (
                jnp.einsum("hqk,khd->qhd", score_grad, keys, preferred_element_type=jnp.float32)
                * factor
            )
            key_grad = (
                key_grad
                + jnp.einsum("hqk,qhd->khd", score_grad, rows_q, preferred_element_type=jnp.float32)
                * factor
            )
            return ((key_grad, value_grad), query_grad)

        zeros = jnp.zeros(keys.shape, jnp.float32)
        (key_grad, value_grad), query_grad = lax.scan(per_block, (zeros, zeros), jnp.arange(count))
        return (query_grad.reshape(length, keys.shape[1], keys.shape[2]), key_grad, value_grad)

    return lax.map(per_sequence, (query4, key4, value4, segments, logsum, grad4))


def body(
    tokens,
    segments,
    w_query,
    w_key,
    w_value,
    w_out,
    w_fc1,
    w_fc2,
    ln1_gain,
    ln1_bias,
    post_gain,
    post_bias,
    ln2_gain,
    ln2_bias,
    mid_gain,
    mid_bias,
    query_bias,
    value_bias,
    out_bias,
    fc1_bias,
    fc2_bias,
    head_scale,
    cotangent,
):
    rows = tokens.shape[0]
    seqs = segments.shape[0]
    length = segments.shape[1]
    block = min(512, length)
    heads = w_query.shape[1] // HEAD_DIM
    shape4 = (seqs, length, heads, HEAD_DIM)
    resid = tokens.astype(jnp.float32)
    normed1, factor1 = normalize(resid)
    entry = (normed1 * ln1_gain + ln1_bias).astype(jnp.bfloat16)
    query = (project(entry, w_query) + query_bias).astype(jnp.bfloat16)
    keyed = project(entry, w_key).astype(jnp.bfloat16)
    valued = (project(entry, w_value) + value_bias).astype(jnp.bfloat16)
    query4 = query.reshape(shape4)
    key4 = keyed.reshape(shape4)
    value4 = valued.reshape(shape4)
    attended, logsum = attend(query4, key4, value4, segments, block)
    attended = attended.reshape(rows, heads, HEAD_DIM)
    context = (attended * head_scale[:, None]).reshape(rows, heads * HEAD_DIM).astype(jnp.bfloat16)
    mixed = lax.psum(project_t(context, w_out), "tensor") + out_bias
    normedp, factorp = normalize(mixed)
    branch = normedp * post_gain + post_bias
    stream = resid + branch
    normed2, factor2 = normalize(stream)
    inner = (normed2 * ln2_gain + ln2_bias).astype(jnp.bfloat16)
    hidden = project(inner, w_fc1) + fc1_bias
    active, gelu_pull = jax.vjp(gelu_tanh, hidden)
    mean = lax.psum(jnp.sum(active, axis=-1, keepdims=True), "tensor") / FF
    centred = active - mean
    spread = lax.psum(jnp.sum(centred * centred, axis=-1, keepdims=True), "tensor") / FF
    factorm = lax.rsqrt(spread + epsilon)
    normedm = centred * factorm
    middle = (normedm * mid_gain + mid_bias).astype(jnp.bfloat16)
    ffn_out = lax.psum(project_t(middle, w_fc2), "tensor") + fc2_bias
    result = stream + ffn_out
    output = result.astype(jnp.bfloat16)
    upstream = cotangent.astype(jnp.float32)
    grad_fc2_bias = jnp.sum(upstream, axis=0)
    grad_w_fc2 = outer_sum(cotangent, middle)
    grad_middle = project(cotangent, w_fc2)
    grad_mid_gain = jnp.sum(grad_middle * normedm, axis=0)
    grad_mid_bias = jnp.sum(grad_middle, axis=0)
    scaled = grad_middle * mid_gain
    sum_plain, sum_normed = lax.psum(
        (
            jnp.sum(scaled, axis=-1, keepdims=True),
            jnp.sum(scaled * normedm, axis=-1, keepdims=True),
        ),
        "tensor",
    )
    grad_active = factorm * (scaled - sum_plain / FF - normedm * (sum_normed / FF))
    grad_hidden = gelu_pull(grad_active)[0].astype(jnp.bfloat16)
    grad_fc1_bias = jnp.sum(grad_hidden.astype(jnp.float32), axis=0)
    grad_w_fc1 = outer_sum(inner, grad_hidden)
    grad_inner = lax.psum(project_t(grad_hidden, w_fc1), "tensor")
    grad_ln2_gain = jnp.sum(grad_inner * normed2, axis=0)
    grad_ln2_bias = jnp.sum(grad_inner, axis=0)
    grad_stream = upstream + norm_back(grad_inner * ln2_gain, normed2, factor2)
    grad_post_gain = jnp.sum(grad_stream * normedp, axis=0)
    grad_post_bias = jnp.sum(grad_stream, axis=0)
    grad_mixed = norm_back(grad_stream * post_gain, normedp, factorp).astype(jnp.bfloat16)
    grad_out_bias = jnp.sum(grad_mixed.astype(jnp.float32), axis=0)
    grad_w_out = outer_sum(grad_mixed, context)
    grad_context = project(grad_mixed, w_out).reshape(rows, heads, HEAD_DIM)
    grad_head = jnp.sum(grad_context * attended, axis=(0, 2))
    grad_attended = (grad_context * head_scale[:, None]).astype(jnp.bfloat16)
    grad_q4, grad_k4, grad_v4 = attend_back(
        query4, key4, value4, segments, logsum, grad_attended.reshape(shape4), block
    )
    grad_query = grad_q4.reshape(rows, heads * HEAD_DIM).astype(jnp.bfloat16)
    grad_key = grad_k4.reshape(rows, heads * HEAD_DIM).astype(jnp.bfloat16)
    grad_value = grad_v4.reshape(rows, heads * HEAD_DIM).astype(jnp.bfloat16)
    grad_query_bias = jnp.sum(grad_query.astype(jnp.float32), axis=0)
    grad_value_bias = jnp.sum(grad_value.astype(jnp.float32), axis=0)
    grad_w_query = outer_sum(entry, grad_query)
    grad_w_key = outer_sum(entry, grad_key)
    grad_w_value = outer_sum(entry, grad_value)
    grad_entry = lax.psum(
        project_t(grad_query, w_query)
        + project_t(grad_key, w_key)
        + project_t(grad_value, w_value),
        "tensor",
    )
    grad_ln1_gain = jnp.sum(grad_entry * normed1, axis=0)
    grad_ln1_bias = jnp.sum(grad_entry, axis=0)
    grad_tokens = grad_stream + norm_back(grad_entry * ln1_gain, normed1, factor1)
    valid = (segments >= 0).reshape(rows, 1).astype(jnp.float32)
    squares = jnp.stack(
        [
            jnp.sum(valid * branch * branch),
            jnp.sum(valid * ffn_out * ffn_out),
            jnp.sum(valid * result * result),
        ]
    )
    counted = jnp.sum(valid)
    (
        grad_ln1_gain,
        grad_ln1_bias,
        grad_post_gain,
        grad_post_bias,
        grad_ln2_gain,
        grad_ln2_bias,
        grad_mid_gain,
        grad_mid_bias,
        grad_query_bias,
        grad_value_bias,
        grad_out_bias,
        grad_fc1_bias,
        grad_fc2_bias,
        grad_head,
        squares,
        counted,
    ) = lax.psum(
        (
            grad_ln1_gain,
            grad_ln1_bias,
            grad_post_gain,
            grad_post_bias,
            grad_ln2_gain,
            grad_ln2_bias,
            grad_mid_gain,
            grad_mid_bias,
            grad_query_bias,
            grad_value_bias,
            grad_out_bias,
            grad_fc1_bias,
            grad_fc2_bias,
            grad_head,
            squares,
            counted,
        ),
        "dp",
    )
    rms = jnp.sqrt(squares / (counted * D))
    grad_w_query, grad_w_key, grad_w_value, grad_w_out, grad_w_fc1, grad_w_fc2 = (
        lax.psum_scatter(grad_w_query, "dp", scatter_dimension=0, tiled=True),
        lax.psum_scatter(grad_w_key, "dp", scatter_dimension=0, tiled=True),
        lax.psum_scatter(grad_w_value, "dp", scatter_dimension=0, tiled=True),
        lax.psum_scatter(grad_w_out, "dp", scatter_dimension=0, tiled=True),
        lax.psum_scatter(grad_w_fc1, "dp", scatter_dimension=0, tiled=True),
        lax.psum_scatter(grad_w_fc2, "dp", scatter_dimension=0, tiled=True),
    )
    return (
        output,
        grad_tokens,
        grad_w_query,
        grad_w_key,
        grad_w_value,
        grad_w_out,
        grad_w_fc1,
        grad_w_fc2,
        grad_ln1_gain,
        grad_ln1_bias,
        grad_post_gain,
        grad_post_bias,
        grad_ln2_gain,
        grad_ln2_bias,
        grad_mid_gain,
        grad_mid_bias,
        grad_query_bias,
        grad_value_bias,
        grad_out_bias,
        grad_fc1_bias,
        grad_fc2_bias,
        grad_head,
        rms,
    )


def solution(mesh):
    return jax.shard_map(
        body,
        mesh=mesh,
        in_specs=(
            P("dp", None),
            P("dp", None),
            P(None, "tensor"),
            P(None, "tensor"),
            P(None, "tensor"),
            P(None, "tensor"),
            P(None, "tensor"),
            P(None, "tensor"),
            P(),
            P(),
            P(),
            P(),
            P(),
            P(),
            P("tensor"),
            P("tensor"),
            P("tensor"),
            P("tensor"),
            P(),
            P("tensor"),
            P(),
            P("tensor"),
            P("dp", None),
        ),
        out_specs=(
            P("dp", None),
            P("dp", None),
            P("dp", "tensor"),
            P("dp", "tensor"),
            P("dp", "tensor"),
            P("dp", "tensor"),
            P("dp", "tensor"),
            P("dp", "tensor"),
            P(),
            P(),
            P(),
            P(),
            P(),
            P(),
            P("tensor"),
            P("tensor"),
            P("tensor"),
            P("tensor"),
            P(),
            P("tensor"),
            P(),
            P("tensor"),
            P(),
        ),
        check_vma=False,
    )
```

profile of v0, /device:TPU:0, one launch (start us, length us, event | category | flops | bytes accessed | tf_op | source)
XLA Modules:
  0.0 981.3 jit_solution(746196354005105888)
XLA Ops:
  17.5 42.9 %while.47 = (s32[]{:T(128)}, f32[2,512,4,64]{1,0,3,2:T(2,128)}, f32[2,4,512]{2,1,0:T(4,128)S(1)}, s32[2]{0:T(128)S(1)}, s32[1024]{0:T(1024)S(1)}, /*index=5*/bf1...) while((s32[]{:T(128)}, f32[2,512,4,64]{1,0,3,2:T(2,128)}, ...), condition=%wide.region_5.6_spmd, body=%wide.region_2.5_spmd.sunk | while | flops 563608064 | bytes 31275212 | solution.py:77
  19.5 2.6 fusion.140
  22.1 2.3 fusion.141
  24.4 3.6 fusion.142
  28.6 10.4 %dynamic_update_slice.30 = f32[2,512,4,64]{1,0,3,2:T(2,128)} dynamic-update-slice(f32[2,512,4,64]{1,0,3,2:T(2,128)} %get-tuple-element.525, f32[1,512,4,64]{1,0,3,2:T(1,128)S(1)} %copy.100, s32[]{:T(128)S(6)} %copy.107, s32[]{:T(128)} %constant.111.clone.1..sunk, s32[]{:T(128)} %constant.111.clone.1..sunk, s32[]{:T(128)} %constant.111.clone.1..sunk) | dynamic-update-slice | bytes 1048580 | tf_op jit(solution)/shard_map/while/body/eval_jaxpr/while/body/jit(dynamic_update_index_in_dim)/dynamic_update_slice | solution.py:77
  40.9 2.6 fusion.140
  45.9 3.6 fusion.142
  50.0 10.4 %dynamic_update_slice.30 = f32[2,512,4,64]{1,0,3,2:T(2,128)} dynamic-update-slice(f32[2,512,4,64]{1,0,3,2:T(2,128)} %get-tuple-element.525, f32[1,512,4,64]{1,0,3,2:T(1,128)S(1)} %copy.100, s32[]{:T(128)S(6)} %copy.107, s32[]{:T(128)} %constant.111.clone.1..sunk, s32[]{:T(128)} %constant.111.clone.1..sunk, s32[]{:T(128)} %constant.111.clone.1..sunk) | dynamic-update-slice | bytes 1048580 | tf_op jit(solution)/shard_map/while/body/eval_jaxpr/while/body/jit(dynamic_update_index_in_dim)/dynamic_update_slice | solution.py:77
  62.9 3.9 fusion.66
  67.1 6.4 fusion.73
  73.5 5.3 copy.56
  78.9 76.3 %all-reduce.7.cloned.1.call-done = f32[1024,1024]{1,0:T(8,128)} async-done(((f32[1024,1024]{1,0:T(8,128)}), f32[1024,1024]{1,0:T(8,128)}) %all-reduce.7.cloned.1.call-update) | async-done | bytes 4194320 | tf_op jit(solution)/shard_map/psum | solution.py:169
  155.2 2.7 add_reduce_fusion
  161.9 2.4 copy-done.62
  164.3 5.5 fusion.70
  169.8 6.0 psum.169
  175.8 3.7 multiply_reduce_fusion.7
  179.4 6.1 psum.170
  185.5 8.0 fusion.67
  193.6 3.7 multiply_reduce_fusion.1
  197.2 6.1 all-reduce.1
  203.4 8.0 convert_reduce_fusion.2
  211.5 4.4 fusion.74
  216.1 153.8 %all-reduce.11.cloned.1.call-done = (f32[1024,1024]{1,0:T(8,128)}, f32[1024,1024]{1,0:T(8,128)}) async-done(((f32[1024,1024]{1,0:T(8,128)}, f32[1024,1024]{1,0:T(8,128)}), (f32[1024,1024]{1,0:T(8,128)}, f32[1024,1024]{1,0:T(8,128)})) %all-reduce.11.cloned.1.call-update) | async-done | bytes 8388624 | tf_op jit(solution)/shard_map/psum | solution.py:183
  370.0 8.2 fusion.59
  379.6 6.3 multiply_reduce_fusion.3
  390.2 38.5 %while.48 = (s32[]{:T(128)}, f32[1024,4,64]{0,2,1:T(8,128)S(1)}, f32[1024,4,64]{0,2,1:T(8,128)}, bf16[2,512,4,64]{1,3,2,0:T(8,128)(2,1)S(1)}, s32[2]{0:T(128)S(1...) while((s32[]{:T(128)}, f32[1024,4,64]{0,2,1:T(8,128)S(1)}, ...), condition=%wide.region_27.28_spmd.clone, body=%wide.region_25.27_spmd.clone.sunk | while | flops 1376647680 | bytes 80812376 | solution.py:120
  396.5 2.6 fusion.155
  399.0 4.6 multiply_reduce_fusion.16
  403.6 2.4 multiply_convert_fusion.8
  415.6 2.6 fusion.155
  418.2 4.6 multiply_reduce_fusion.16
  422.8 2.4 multiply_convert_fusion.8
  432.2 2.7 add_add_fusion
  436.6 7.9 convolution_bitcast_fusion
  445.7 3.5 fusion.65
  449.3 3.0 fusion.79
  456.2 7.6 fusion.68
  467.4 53.4 %all-reduce.9.cloned.1.call-done = f32[1024,1024]{1,0:T(8,128)} async-done(((f32[1024,1024]{1,0:T(8,128)}), f32[1024,1024]{1,0:T(8,128)}) %all-reduce.9.cloned.1.call-update) | async-done | bytes 4194320 | tf_op jit(solution)/shard_map/psum | solution.py:227
  520.8 3.7 fusion.49
  524.6 40.9 %all-reduce = (f32[1024]{0:T(1024)}, f32[1024]{0:T(1024)}, f32[1024]{0:T(1024)}, f32[1024]{0:T(1024)}, f32[1024]{0:T(1024)}, /*index=5*/f32[1024]{0:T(1024)}, f3...) all-reduce(f32[1024]{0:T(1024)S(1)} %get-tuple-element.292, ...), channel_id=1, replica_groups=mesh['dp'=8,'tensor'=4] {'dp'}, use_global_device_ids=true, to_apply=%region_38.39 | all-reduce | flops 11784 | bytes 94272 | tf_op jit(solution)/shard_map/psum | solution.py:262
  566.6 6.4 fusion.48
  573.1 40.9 %reduce-scatter.17.cloned.1.call-done = f32[128,1024]{0,1:T(8,128)} async-done(((f32[1024,1024]{0,1:T(8,128)}), f32[128,1024]{0,1:T(8,128)}) %reduce-scatter.17.cloned.1.call-update) | async-done | bytes 524304 | tf_op jit(solution)/shard_map/reduce_scatter | solution.py:290
  616.0 65.7 %reduce-scatter.13.cloned.1.call-done = f32[128,256]{1,0:T(8,128)} async-done(((f32[1024,256]{1,0:T(8,128)}), f32[128,256]{1,0:T(8,128)}) %reduce-scatter.13.cloned.1.call-update) | async-done | bytes 131088 | tf_op jit(solution)/shard_map/reduce_scatter | solution.py:288
  681.7 67.0 %reduce-scatter.11.cloned.1.call-done = f32[128,256]{1,0:T(8,128)} async-done(((f32[1024,256]{1,0:T(8,128)}), f32[128,256]{1,0:T(8,128)}) %reduce-scatter.11.cloned.1.call-update) | async-done | bytes 131088 | tf_op jit(solution)/shard_map/reduce_scatter | solution.py:287
  748.7 67.1 %reduce-scatter.9.cloned.1.call-done = f32[128,256]{1,0:T(8,128)} async-done(((f32[1024,256]{1,0:T(8,128)}), f32[128,256]{1,0:T(8,128)}) %reduce-scatter.9.cloned.1.call-update) | async-done | bytes 131088 | tf_op jit(solution)/shard_map/reduce_scatter | solution.py:286
  815.8 67.1 %reduce-scatter.7.cloned.1.call-done = f32[128,256]{1,0:T(8,128)} async-done(((f32[1024,256]{1,0:T(8,128)}), f32[128,256]{1,0:T(8,128)}) %reduce-scatter.7.cloned.1.call-update) | async-done | bytes 131088 | tf_op jit(solution)/shard_map/reduce_scatter | solution.py:285
  882.9 91.5 %reduce-scatter.15.cloned.1.call-done = f32[128,1024]{1,0:T(8,128)} async-done(((f32[1024,1024]{1,0:T(8,128)}), f32[128,1024]{1,0:T(8,128)}) %reduce-scatter.15.cloned.1.call-update) | async-done | bytes 524304 | tf_op jit(solution)/shard_map/reduce_scatter | solution.py:289
  (243 shorter events, 58.8 us)
Async XLA Ops:
  7.2 59.9 %copy-start = (bf16[1024,1024]{1,0:T(8,128)(2,1)S(1)}, bf16[1024,1024]{1,0:T(8,128)(2,1)}, u32[]{:S(2)}) copy-start(bf16[1024,1024]{1,0:T(8,128)(2,1)} %param.34) | copy-start | bytes 6291460
  7.2 5.5 copy-start.46
  7.2 5.5 copy-start.60
  7.2 148.0 %all-reduce.7.cloned.1.call-start = ((), (), s32[]{:S(2)}) async-start(), calls=%async_computation.6 | async-start | bytes 8388608 | tf_op jit(solution)/shard_map/psum | solution.py:169
  8.2 53.6 %copy-start.56 = (f32[256]{0:T(256)}, f32[256]{0:T(256)S(1)}, u32[]{:S(2)}) copy-start(f32[256]{0:T(256)S(1)} %mul.324) | copy-start | bytes 3076
  8.2 4.4 copy-start.4
  8.2 5.3 copy-start.34
  10.3 4.0 copy-start.40
  13.5 4.0 copy-start.9
  66.8 303.1 %all-reduce.11.cloned.1.call-start = ((), (), s32[]{:S(2)}) async-start(), calls=%async_computation.14 | async-start | bytes 16777216 | tf_op jit(solution)/shard_map/psum | solution.py:183
  73.5 81.7 %copy-start.42 = (f32[1024]{0:T(1024)S(1)}, f32[1024]{0:T(1024)}, u32[]{:S(2)}) copy-start(f32[1024]{0:T(1024)} %param.45) | copy-start | bytes 12292
  78.9 80.5 %copy-start.48 = (f32[1024]{0:T(1024)S(1)}, f32[1024]{0:T(1024)}, u32[]{:S(2)}) copy-start(f32[1024]{0:T(1024)} %param.37) | copy-start | bytes 12292
  78.9 80.5 %copy-start.54 = (f32[1024]{0:T(1024)S(1)}, f32[1024]{0:T(1024)}, u32[]{:S(2)}) copy-start(f32[1024]{0:T(1024)} %param.38) | copy-start | bytes 12292
  155.2 3.4 copy-start.2
  155.2 4.2 copy-start.5
  161.1 8.6 copy-start.7
  169.8 15.7 %copy-start.49 = (f32[1024]{0:T(1024)S(1)}, f32[1024]{0:T(1024)}, u32[]{:S(2)}) copy-start(f32[1024]{0:T(1024)} %param.41) | copy-start | bytes 12292
  169.8 15.8 %copy-start.64 = (f32[1024]{0:T(1024)S(1)}, f32[1024]{0:T(1024)}, u32[]{:S(2)}) copy-start(f32[1024]{0:T(1024)} %param.42) | copy-start | bytes 12292
  185.5 8.1 copy-start.12
  185.5 8.0 copy-start.13
  203.4 8.1 copy-start.63
  211.5 4.4 copy-start.27
  215.8 154.1 %copy-start.58 = (f32[1024]{0:T(1024)S(1)}, f32[1024]{0:T(1024)}, u32[]{:S(2)}) copy-start(f32[1024]{0:T(1024)} %param.47) | copy-start | bytes 12292
  215.9 304.9 %all-reduce.9.cloned.1.call-start = ((), (), s32[]{:S(2)}) async-start(), calls=%async_computation.7 | async-start | bytes 8388608 | tf_op jit(solution)/shard_map/psum | solution.py:227
  369.9 8.2 copy-start.3
  369.9 8.2 copy-start.8
  370.0 9.1 copy-start.18
  370.0 9.7 copy-start.28
  385.9 3.3 copy-start.16
  399.0 4.6 copy-start.32
  418.2 4.6 copy-start.32
  435.0 179.0 %reduce-scatter.17.cloned.1.call-start = ((), (), s32[]{:S(2)}) async-start(), calls=%async_computation.13 | async-start | bytes 4718592 | tf_op jit(solution)/shard_map/reduce_scatter | solution.py:290
  444.5 4.8 copy-start.10
  444.5 237.1 %reduce-scatter.13.cloned.1.call-start = ((), (), s32[]{:S(2)}) async-start(), calls=%async_computation.11 | async-start | bytes 1179648 | tf_op jit(solution)/shard_map/reduce_scatter | solution.py:288
  449.2 299.4 %reduce-scatter.11.cloned.1.call-start = ((), (), s32[]{:S(2)}) async-start(), calls=%async_computation.10 | async-start | bytes 1179648 | tf_op jit(solution)/shard_map/reduce_scatter | solution.py:287
  452.3 363.5 %reduce-scatter.9.cloned.1.call-start = ((), (), s32[]{:S(2)}) async-start(), calls=%async_computation.9 | async-start | bytes 1179648 | tf_op jit(solution)/shard_map/reduce_scatter | solution.py:286
  454.1 428.8 %reduce-scatter.7.cloned.1.call-start = ((), (), s32[]{:S(2)}) async-start(), calls=%async_computation.8 | async-start | bytes 1179648 | tf_op jit(solution)/shard_map/reduce_scatter | solution.py:285
  455.9 518.4 %reduce-scatter.15.cloned.1.call-start = ((), (), s32[]{:S(2)}) async-start(), calls=%async_computation.12 | async-start | bytes 4718592 | tf_op jit(solution)/shard_map/reduce_scatter | solution.py:289
  463.8 56.9 %copy-start.6 = (bf16[1024,1024]{1,0:T(8,128)(2,1)S(1)}, bf16[1024,1024]{1,0:T(8,128)(2,1)}, u32[]{:S(2)}) copy-start(bf16[1024,1024]{1,0:T(8,128)(2,1)} %param.27) | copy-start | bytes 6291460
  463.8 56.9 %copy-start.41 = (f32[1024]{0:T(1024)S(1)}, f32[1024]{0:T(1024)}, u32[]{:S(2)}) copy-start(f32[1024]{0:T(1024)} %copy-done.40) | copy-start | bytes 12292
  463.8 56.9 %copy-start.44 = (f32[1024]{0:T(1024)S(1)}, f32[1024]{0:T(1024)}, u32[]{:S(2)}) copy-start(f32[1024]{0:T(1024)} %copy-done.43) | copy-start | bytes 12292
  463.9 56.9 %copy-start.47 = (f32[1024]{0:T(1024)S(1)}, f32[1024]{0:T(1024)}, u32[]{:S(2)}) copy-start(f32[1024]{0:T(1024)} %param.35) | copy-start | bytes 12292
  463.9 60.6 %copy-start.50 = (f32[1024]{0:T(1024)S(1)}, f32[1024]{0:T(1024)}, u32[]{:S(2)}) copy-start(f32[1024]{0:T(1024)} %get-tuple-element.286) | copy-start | bytes 12292
  463.9 60.6 %copy-start.51 = (f32[1024]{0:T(1024)S(1)}, f32[1024]{0:T(1024)}, u32[]{:S(2)}) copy-start(f32[1024]{0:T(1024)} %get-tuple-element.365) | copy-start | bytes 12292
  463.9 60.6 %copy-start.52 = (f32[1024]{0:T(1024)S(1)}, f32[1024]{0:T(1024)}, u32[]{:S(2)}) copy-start(f32[1024]{0:T(1024)} %get-tuple-element.303) | copy-start | bytes 12292
  463.9 60.6 %copy-start.53 = (f32[1024]{0:T(1024)S(1)}, f32[1024]{0:T(1024)}, u32[]{:S(2)}) copy-start(f32[1024]{0:T(1024)} %get-tuple-element.304) | copy-start | bytes 12292
  463.9 60.6 %copy-start.59 = (f32[1024]{0:T(1024)S(1)}, f32[1024]{0:T(1024)}, u32[]{:S(2)}) copy-start(f32[1024]{0:T(1024)} %get-tuple-element.382) | copy-start | bytes 12292
  566.6 407.7 %copy-start.1 = (bf16[1024,1024]{1,0:T(8,128)(2,1)S(1)}, bf16[1024,1024]{1,0:T(8,128)(2,1)}, u32[]{:S(2)}) copy-start(bf16[1024,1024]{1,0:T(8,128)(2,1)} %param.34) | copy-start | bytes 6291460
  (32 other events, 66.1 us)
Sparse Core Ops, SparseCore 0:
  66.9 88.1 all-reduce.6
  216.0 153.9 all-reduce.10
  435.1 85.5 all-reduce.8
  524.3 89.6 reduce-scatter.16
  617.8 63.8 reduce-scatter.12
  685.5 63.1 reduce-scatter.10
  752.6 63.1 reduce-scatter.8
  819.8 63.0 reduce-scatter.6
  887.1 87.2 reduce-scatter.14
where the time goes:
time: 992 us; the launch traced here: 981 us
  waiting for transfers between devices  683 us (69%)
  matrix products  101 us (10%)
  other arithmetic  68.1 us (7%)
  blocking collectives  59.1 us (6%)
  local copies, waits for them, and re-layouts  46.8 us (5%)
  between operations  15.8 us (2%)
    psum x1, waiting for transfers between devices, body(): ffn_out = lax.psum(project_t(middle, w_fc2), 'tensor') + fc2_bias  154 us
    reduce_scatter x1, waiting for transfers between devices, body(): lax.psum_scatter(grad_w_fc1, 'dp', scatter_dimension=0, tiled=True)  91.5 us
    psum x1, waiting for transfers between devices, body(): mixed = lax.psum(project_t(context, w_out), 'tensor') + out_bias  76.3 us
    reduce_scatter x1, waiting for transfers between devices, body(): lax.psum_scatter(grad_w_key, 'dp', scatter_dimension=0, tiled=True)  67.1 us
    reduce_scatter x1, waiting for transfers between devices, body(): lax.psum_scatter(grad_w_query, 'dp', scatter_dimension=0, tiled=True)  67.1 us
    reduce_scatter x1, waiting for transfers between devices, body(): lax.psum_scatter(grad_w_value, 'dp', scatter_dimension=0, tiled=True)  67 us
    reduce_scatter x1, waiting for transfers between devices, body(): lax.psum_scatter(grad_w_out, 'dp', scatter_dimension=0, tiled=True)  65.7 us
    psum x1, waiting for transfers between devices, body(): lax.psum(project_t(grad_query, w_query) + project_t(grad_key, w_key) + pr...  53.4 us
  transfers between devices with their start and end apart: 9, of which 9 were waited for; matrix products, arithmetic and copies ran while one was open for 5% of the time, Pallas kernels for 0%

commit v1 on v0

--- a/solution.py
+++ b/solution.py
@@ -2,11 +2,17 @@
 import jax.numpy as jnp
 from jax import lax
 from jax.sharding import PartitionSpec as P
+from jax.lax import all_gather
 
 D = 1024
 HEAD_DIM = 64
 FF = 4096
 epsilon = 1e-05
+
+
+def cut_masks_now(field):
+    tall = all_gather(field, "tensor")
+    return jnp.sum(tall, axis=0)
 
 
 def normalize(v):
@@ -180,7 +186,7 @@
     factorm = lax.rsqrt(spread + epsilon)
     normedm = centred * factorm
     middle = (normedm * mid_gain + mid_bias).astype(jnp.bfloat16)
-    ffn_out = lax.psum(project_t(middle, w_fc2), "tensor") + fc2_bias
+    ffn_out = cut_masks_now(project_t(middle, w_fc2)) + fc2_bias
     result = stream + ffn_out
     output = result.astype(jnp.bfloat16)
     upstream = cotangent.astype(jnp.float32)

time: 992 us -> 948 us (0.956)
  waiting for transfers between devices: 683 us -> 622 us
  other arithmetic: 68.1 us -> 82.3 us
    psum x1, waiting for transfers between devices: 154 us -> 77.5 us  [body(): grad_inner = lax.psum(project_t(grad_hidden, w_fc1), 'tensor')]
    all_gather x0 -> x1, waiting for transfers between devices: none -> 58.6 us  [cut_masks_now(): tall = all_gather(field, 'tensor')]
    reduce_scatter x1, waiting for transfers between devices: 91.5 us -> 41.3 us  [body(): lax.psum_scatter(grad_w_fc1, 'dp', scatter_dimension=0, tiled=True)]
    reduce_scatter x1, waiting for transfers between devices: 40.9 us -> 4.58 us  [body(): lax.psum_scatter(grad_w_fc2, 'dp', scatter_dimension=0, tiled=True)]
    psum x1, waiting for transfers between devices: 53.4 us -> 82.8 us  [body(): lax.psum(project_t(grad_query, w_query) + project_t(grad_key, w_key) + pr...]
    psum x1, waiting for transfers between devices: 76.3 us -> 88.1 us  [body(): mixed = lax.psum(project_t(context, w_out), 'tensor') + out_bias]
    reduce_sum x0 -> x1, other arithmetic: none -> 10.4 us  [cut_masks_now(): return jnp.sum(tall, axis=0)]
  transfers between devices with their start and end apart: 9 -> 10, of which waited for: 9 -> 10; matrix products, arithmetic and copies ran while one was open for 5% -> 15% of each run, Pallas kernels for 0% -> 0%
where the time goes in v1:
time: 948 us; the launch traced here: 937 us
  waiting for transfers between devices  622 us (66%)
  matrix products  102 us (11%)
  other arithmetic  82.3 us (9%)
  blocking collectives  59.2 us (6%)
  local copies, waits for them, and re-layouts  47 us (5%)
  between operations  16.1 us (2%)
    psum x1, waiting for transfers between devices, body(): mixed = lax.psum(project_t(context, w_out), 'tensor') + out_bias  88.1 us
    psum x1, waiting for transfers between devices, body(): lax.psum(project_t(grad_query, w_query) + project_t(grad_key, w_key) + pr...  82.8 us
    psum x1, waiting for transfers between devices, body(): grad_inner = lax.psum(project_t(grad_hidden, w_fc1), 'tensor')  77.5 us
    reduce_scatter x1, waiting for transfers between devices, body(): lax.psum_scatter(grad_w_out, 'dp', scatter_dimension=0, tiled=True)  67.8 us
    reduce_scatter x1, waiting for transfers between devices, body(): lax.psum_scatter(grad_w_key, 'dp', scatter_dimension=0, tiled=True)  67.1 us
    reduce_scatter x1, waiting for transfers between devices, body(): lax.psum_scatter(grad_w_value, 'dp', scatter_dimension=0, tiled=True)  67.1 us
    reduce_scatter x1, waiting for transfers between devices, body(): lax.psum_scatter(grad_w_query, 'dp', scatter_dimension=0, tiled=True)  67 us
    all_gather x1, waiting for transfers between devices, cut_masks_now(): tall = all_gather(field, 'tensor')  58.6 us
  transfers between devices with their start and end apart: 10, of which 10 were waited for; matrix products, arithmetic and copies ran while one was open for 15% of the time, Pallas kernels for 0%

profile of v1, /device:TPU:0, one launch (start us, length us, event | category | flops | bytes accessed | tf_op | source)
XLA Modules:
  0.0 937.4 jit_solution(8013501640030070797)
XLA Ops:
  17.5 42.9 %while.47 = (s32[]{:T(128)}, f32[2,512,4,64]{1,0,3,2:T(2,128)}, f32[2,4,512]{2,1,0:T(4,128)S(1)}, s32[2]{0:T(128)S(1)}, s32[1024]{0:T(1024)S(1)}, /*index=5*/bf1...) while((s32[]{:T(128)}, f32[2,512,4,64]{1,0,3,2:T(2,128)}, ...), condition=%wide.region_5.6_spmd, body=%wide.region_2.5_spmd.sunk | while | flops 563608064 | bytes 31275212 | solution.py:83
  19.5 2.6 fusion.140
  24.4 3.6 fusion.142
  28.6 10.4 %dynamic_update_slice.30 = f32[2,512,4,64]{1,0,3,2:T(2,128)} dynamic-update-slice(f32[2,512,4,64]{1,0,3,2:T(2,128)} %get-tuple-element.523, f32[1,512,4,64]{1,0,3,2:T(1,128)S(1)} %copy.101, s32[]{:T(128)S(6)} %copy.108, s32[]{:T(128)} %constant.111.clone.1..sunk, s32[]{:T(128)} %constant.111.clone.1..sunk, s32[]{:T(128)} %constant.111.clone.1..sunk) | dynamic-update-slice | bytes 1048580 | tf_op jit(solution)/shard_map/while/body/eval_jaxpr/while/body/jit(dynamic_update_index_in_dim)/dynamic_update_slice | solution.py:83
  40.9 2.6 fusion.140
  45.9 3.6 fusion.142
  50.0 10.4 %dynamic_update_slice.30 = f32[2,512,4,64]{1,0,3,2:T(2,128)} dynamic-update-slice(f32[2,512,4,64]{1,0,3,2:T(2,128)} %get-tuple-element.523, f32[1,512,4,64]{1,0,3,2:T(1,128)S(1)} %copy.101, s32[]{:T(128)S(6)} %copy.108, s32[]{:T(128)} %constant.111.clone.1..sunk, s32[]{:T(128)} %constant.111.clone.1..sunk, s32[]{:T(128)} %constant.111.clone.1..sunk) | dynamic-update-slice | bytes 1048580 | tf_op jit(solution)/shard_map/while/body/eval_jaxpr/while/body/jit(dynamic_update_index_in_dim)/dynamic_update_slice | solution.py:83
  62.8 3.9 fusion.66
  67.1 88.1 %all-reduce.6.cloned.1.call-done = f32[1024,1024]{1,0:T(8,128)} async-done(((f32[1024,1024]{1,0:T(8,128)}), f32[1024,1024]{1,0:T(8,128)}) %all-reduce.6.cloned.1.call-update) | async-done | bytes 4194320 | tf_op jit(solution)/shard_map/psum | solution.py:175
  155.1 2.7 add_reduce_fusion
  164.2 5.5 fusion.70
  169.7 6.0 psum.162
  175.7 3.7 multiply_reduce_fusion.7
  179.4 5.7 psum.163
  185.1 7.8 fusion.67
  193.4 6.5 fusion.73
  199.9 5.9 copy.56
  205.8 7.2 multiply_reduce_fusion.1
  213.0 6.8 all-reduce.1
  219.9 8.2 convert_reduce_fusion.2
  228.1 4.4 fusion.74
  232.5 8.6 convolution_bitcast_fusion
  241.4 58.6 %all-gather.3.cloned.1.call-done = f32[4096,1024]{1,0:T(8,128)} async-done(((f32[1024,1024]{1,0:T(8,128)}), f32[4096,1024]{1,0:T(8,128)}) %all-gather.3.cloned.1.call-update) | async-done | bytes 16777232 | tf_op jit(solution)/shard_map/all_gather | solution.py:14
  300.0 10.4 %reduce_sum.352 = f32[1024,1024]{1,0:T(8,128)} reduce(f32[4,1024,1024]{2,1,0:T(8,128)} %bitcast.124, f32[]{:T(128)} %constant.112.clone.1), dimensions={0}, to_apply=%region_15.16 | reduce | flops 3145728 | bytes 20971524 | tf_op jit(solution)/shard_map/reduce_sum | solution.py:15
  310.4 77.5 %all-reduce.8.cloned.1.call-done = f32[1024,1024]{1,0:T(8,128)} async-done(((f32[1024,1024]{1,0:T(8,128)}), f32[1024,1024]{1,0:T(8,128)}) %all-reduce.8.cloned.1.call-update) | async-done | bytes 4194320 | tf_op jit(solution)/shard_map/psum | solution.py:210
  387.9 8.3 fusion.59
  397.6 6.3 multiply_reduce_fusion.3
  408.3 38.8 %while.48 = (s32[]{:T(128)}, f32[1024,4,64]{0,2,1:T(8,128)S(1)}, f32[1024,4,64]{0,2,1:T(8,128)}, bf16[2,512,4,64]{1,3,2,0:T(8,128)(2,1)S(1)}, s32[2]{0:T(128)S(1...) while((s32[]{:T(128)}, f32[1024,4,64]{0,2,1:T(8,128)S(1)}, ...), condition=%wide.region_27.28_spmd.clone, body=%wide.region_25.27_spmd.clone.sunk | while | flops 1376647680 | bytes 80812376 | solution.py:126
  414.7 2.6 fusion.155
  417.3 4.6 multiply_reduce_fusion.16
  421.9 2.4 multiply_convert_fusion.8
  433.9 2.6 fusion.155
  436.4 4.6 multiply_reduce_fusion.16
  450.6 2.8 add_add_fusion
  454.9 6.9 fusion.68
  463.0 3.4 fusion.65
  466.5 2.9 fusion.79
  471.5 3.5 fusion.77
  475.6 4.6 reduce-scatter.17.cloned.1.call-done
  484.8 82.8 %all-reduce.10.cloned.1.call-done = f32[1024,1024]{1,0:T(8,128)} async-done(((f32[1024,1024]{1,0:T(8,128)}), f32[1024,1024]{1,0:T(8,128)}) %all-reduce.10.cloned.1.call-update) | async-done | bytes 4194320 | tf_op jit(solution)/shard_map/psum | solution.py:233
  567.6 3.7 fusion.49
  571.3 40.7 %all-reduce = (f32[1024]{0:T(1024)}, f32[1024]{0:T(1024)}, f32[1024]{0:T(1024)}, f32[1024]{0:T(1024)}, f32[1024]{0:T(1024)}, /*index=5*/f32[1024]{0:T(1024)}, f3...) all-reduce(f32[1024]{0:T(1024)S(1)} %get-tuple-element.292, ...), channel_id=1, replica_groups=mesh['dp'=8,'tensor'=4] {'dp'}, use_global_device_ids=true, to_apply=%region_38.39 | all-reduce | flops 11784 | bytes 94272 | tf_op jit(solution)/shard_map/psum | solution.py:268
  613.2 6.5 fusion.48
  619.7 41.3 %reduce-scatter.15.cloned.1.call-done = f32[128,1024]{1,0:T(8,128)} async-done(((f32[1024,1024]{1,0:T(8,128)}), f32[128,1024]{1,0:T(8,128)}) %reduce-scatter.15.cloned.1.call-update) | async-done | bytes 524304 | tf_op jit(solution)/shard_map/reduce_scatter | solution.py:295
  661.0 67.8 %reduce-scatter.13.cloned.1.call-done = f32[128,256]{1,0:T(8,128)} async-done(((f32[1024,256]{1,0:T(8,128)}), f32[128,256]{1,0:T(8,128)}) %reduce-scatter.13.cloned.1.call-update) | async-done | bytes 131088 | tf_op jit(solution)/shard_map/reduce_scatter | solution.py:294
  728.8 67.1 %reduce-scatter.11.cloned.1.call-done = f32[128,256]{1,0:T(8,128)} async-done(((f32[1024,256]{1,0:T(8,128)}), f32[128,256]{1,0:T(8,128)}) %reduce-scatter.11.cloned.1.call-update) | async-done | bytes 131088 | tf_op jit(solution)/shard_map/reduce_scatter | solution.py:293
  796.0 67.1 %reduce-scatter.9.cloned.1.call-done = f32[128,256]{1,0:T(8,128)} async-done(((f32[1024,256]{1,0:T(8,128)}), f32[128,256]{1,0:T(8,128)}) %reduce-scatter.9.cloned.1.call-update) | async-done | bytes 131088 | tf_op jit(solution)/shard_map/reduce_scatter | solution.py:292
  863.1 67.0 %reduce-scatter.7.cloned.1.call-done = f32[128,256]{1,0:T(8,128)} async-done(((f32[1024,256]{1,0:T(8,128)}), f32[128,256]{1,0:T(8,128)}) %reduce-scatter.7.cloned.1.call-update) | async-done | bytes 131088 | tf_op jit(solution)/shard_map/reduce_scatter | solution.py:291
  (239 shorter events, 64.1 us)
Async XLA Ops:
  7.2 177.9 %copy-start = (bf16[1024,1024]{1,0:T(8,128)(2,1)S(1)}, bf16[1024,1024]{1,0:T(8,128)(2,1)}, u32[]{:S(2)}) copy-start(bf16[1024,1024]{1,0:T(8,128)(2,1)} %param.34) | copy-start | bytes 6291460
  7.2 5.5 copy-start.44
  7.2 5.5 copy-start.56
  7.2 147.9 %all-reduce.6.cloned.1.call-start = ((), (), s32[]{:S(2)}) async-start(), calls=%async_computation.6 | async-start | bytes 8388608 | tf_op jit(solution)/shard_map/psum | solution.py:175
  8.2 53.6 %copy-start.52 = (f32[256]{0:T(256)}, f32[256]{0:T(256)S(1)}, u32[]{:S(2)}) copy-start(f32[256]{0:T(256)S(1)} %mul.324) | copy-start | bytes 3076
  8.2 4.4 copy-start.4
  8.2 5.3 copy-start.32
  10.3 4.0 copy-start.38
  12.7 3.3 copy-start.41
  13.5 4.0 copy-start.9
  62.8 92.3 %copy-start.40 = (f32[1024]{0:T(1024)S(1)}, f32[1024]{0:T(1024)}, u32[]{:S(2)}) copy-start(f32[1024]{0:T(1024)} %param.45) | copy-start | bytes 12292
  66.8 92.5 %copy-start.46 = (f32[1024]{0:T(1024)S(1)}, f32[1024]{0:T(1024)}, u32[]{:S(2)}) copy-start(f32[1024]{0:T(1024)} %param.37) | copy-start | bytes 12292
  66.8 92.5 %copy-start.50 = (f32[1024]{0:T(1024)S(1)}, f32[1024]{0:T(1024)}, u32[]{:S(2)}) copy-start(f32[1024]{0:T(1024)} %param.38) | copy-start | bytes 12292
  66.8 233.2 %all-gather.3.cloned.1.call-start = ((), (), s32[]{:S(2)}) async-start(), calls=%async_computation.15 | async-start | bytes 20971520 | tf_op jit(solution)/shard_map/all_gather | solution.py:14
  155.1 3.4 copy-start.2
  155.1 4.2 copy-start.5
  161.1 8.6 copy-start.7
  169.7 15.4 %copy-start.47 = (f32[1024]{0:T(1024)S(1)}, f32[1024]{0:T(1024)}, u32[]{:S(2)}) copy-start(f32[1024]{0:T(1024)} %param.41) | copy-start | bytes 12292
  169.7 15.4 %copy-start.60 = (f32[1024]{0:T(1024)S(1)}, f32[1024]{0:T(1024)}, u32[]{:S(2)}) copy-start(f32[1024]{0:T(1024)} %param.42) | copy-start | bytes 12292
  193.0 194.9 %all-reduce.8.cloned.1.call-start = ((), (), s32[]{:S(2)}) async-start(), calls=%async_computation.7 | async-start | bytes 8388608 | tf_op jit(solution)/shard_map/psum | solution.py:210
  219.9 8.2 copy-start.59
  228.0 4.4 copy-start.25
  232.4 247.8 %reduce-scatter.17.cloned.1.call-start = ((), (), s32[]{:S(2)}) async-start(), calls=%async_computation.14 | async-start | bytes 4718592 | tf_op jit(solution)/shard_map/reduce_scatter | solution.py:296
  241.2 326.4 %all-reduce.10.cloned.1.call-start = ((), (), s32[]{:S(2)}) async-start(), calls=%async_computation.8 | async-start | bytes 8388608 | tf_op jit(solution)/shard_map/psum | solution.py:233
  300.0 87.9 %copy-start.54 = (f32[1024]{0:T(1024)S(1)}, f32[1024]{0:T(1024)}, u32[]{:S(2)}) copy-start(f32[1024]{0:T(1024)} %param.47) | copy-start | bytes 12292
  387.9 8.3 copy-start.3
  387.9 8.3 copy-start.8
  387.9 9.1 copy-start.16
  387.9 9.7 %copy-start.27 = (bf16[1024,1024]{1,0:T(8,128)(2,1)S(1)}, bf16[1024,1024]{1,0:T(8,128)(2,1)}, u32[]{:S(2)}) copy-start(bf16[1024,1024]{1,0:T(8,128)(2,1)} %param.49) | copy-start | bytes 6291460
  403.9 3.4 copy-start.14
  403.9 3.4 copy-start.22
  417.3 4.6 copy-start.30
  436.4 4.6 copy-start.30
  453.4 207.6 %reduce-scatter.15.cloned.1.call-start = ((), (), s32[]{:S(2)}) async-start(), calls=%async_computation.13 | async-start | bytes 4718592 | tf_op jit(solution)/shard_map/reduce_scatter | solution.py:295
  461.8 4.7 copy-start.10
  461.8 267.0 %reduce-scatter.13.cloned.1.call-start = ((), (), s32[]{:S(2)}) async-start(), calls=%async_computation.12 | async-start | bytes 1179648 | tf_op jit(solution)/shard_map/reduce_scatter | solution.py:294
  466.5 329.5 %reduce-scatter.11.cloned.1.call-start = ((), (), s32[]{:S(2)}) async-start(), calls=%async_computation.11 | async-start | bytes 1179648 | tf_op jit(solution)/shard_map/reduce_scatter | solution.py:293
  469.5 393.6 %reduce-scatter.9.cloned.1.call-start = ((), (), s32[]{:S(2)}) async-start(), calls=%async_computation.10 | async-start | bytes 1179648 | tf_op jit(solution)/shard_map/reduce_scatter | solution.py:292
  471.3 11.2 %copy-start.24 = (bf16[2,512,4,64]{1,3,2,0:T(8,128)(2,1)S(1)}, bf16[2,512,4,64]{1,3,2,0:T(8,128)(2,1)}, u32[]{:S(2)}) copy-start(bf16[2,512,4,64]{1,3,2,0:T(8,128)(2,1)} %copy-done.23) | copy-start | bytes 1572868
  471.3 96.2 %copy-start.6 = (bf16[1024,1024]{1,0:T(8,128)(2,1)S(1)}, bf16[1024,1024]{1,0:T(8,128)(2,1)}, u32[]{:S(2)}) copy-start(bf16[1024,1024]{1,0:T(8,128)(2,1)} %param.27) | copy-start | bytes 6291460
  471.4 96.2 %copy-start.39 = (f32[1024]{0:T(1024)S(1)}, f32[1024]{0:T(1024)}, u32[]{:S(2)}) copy-start(f32[1024]{0:T(1024)} %copy-done.38) | copy-start | bytes 12292
  471.4 96.2 %copy-start.42 = (f32[1024]{0:T(1024)S(1)}, f32[1024]{0:T(1024)}, u32[]{:S(2)}) copy-start(f32[1024]{0:T(1024)} %copy-done.41) | copy-start | bytes 12292
  471.4 96.2 %copy-start.45 = (f32[1024]{0:T(1024)S(1)}, f32[1024]{0:T(1024)}, u32[]{:S(2)}) copy-start(f32[1024]{0:T(1024)} %param.35) | copy-start | bytes 12292
  471.4 458.7 %reduce-scatter.7.cloned.1.call-start = ((), (), s32[]{:S(2)}) async-start(), calls=%async_computation.9 | async-start | bytes 1179648 | tf_op jit(solution)/shard_map/reduce_scatter | solution.py:291
  475.0 96.3 %copy-start.48 = (f32[1024]{0:T(1024)S(1)}, f32[1024]{0:T(1024)}, u32[]{:S(2)}) copy-start(f32[1024]{0:T(1024)} %get-tuple-element.286) | copy-start | bytes 12292
  475.0 96.3 %copy-start.49 = (f32[1024]{0:T(1024)S(1)}, f32[1024]{0:T(1024)}, u32[]{:S(2)}) copy-start(f32[1024]{0:T(1024)} %get-tuple-element.363) | copy-start | bytes 12292
  475.0 96.3 %copy-start.55 = (f32[1024]{0:T(1024)S(1)}, f32[1024]{0:T(1024)}, u32[]{:S(2)}) copy-start(f32[1024]{0:T(1024)} %get-tuple-element.380) | copy-start | bytes 12292
  613.2 316.9 %copy-start.1 = (bf16[1024,1024]{1,0:T(8,128)(2,1)S(1)}, bf16[1024,1024]{1,0:T(8,128)(2,1)}, u32[]{:S(2)}) copy-start(bf16[1024,1024]{1,0:T(8,128)(2,1)} %param.34) | copy-start | bytes 6291460
  (29 other events, 58.0 us)
Sparse Core Ops, SparseCore 0:
  66.9 88.1 all-reduce.5
  193.1 106.8 all-gather.2
  302.4 85.4 all-reduce.7
  391.4 88.8 reduce-scatter.16
  482.4 85.1 all-reduce.9
  571.6 89.3 reduce-scatter.14
  665.0 63.8 reduce-scatter.12
  732.8 63.1 reduce-scatter.10
  800.0 63.1 reduce-scatter.8
  866.9 63.1 reduce-scatter.6
